TPU v7x, 32 devices: a whole 2x2x4 slice. The times are simulated.
32 devices in a mesh: ens: 2 (over y), grid: 4 (over z), pole: 4 (over x, core).
Axes of the slice: x: 2, y: 2, z: 4, core: 2. Of those that a mesh axis runs over, the one named last changes fastest.
Arguments:
- inverse_pool: bfloat16 [8, 2, 4096, 4096], P(('ens', 'pole'), None, 'grid'), parts along dimension 0, may hold values from -6 to 6
- factor_tiles: bfloat16 [8, 4, 2, 10, 256, 256], P(('ens', 'pole'), None, None, None, 'grid'), parts along dimension 0, may hold values from -0.078125 to 0.078125
- diag_inverse: bfloat16 [8, 2, 1024, 256], P(('ens', 'pole'), None, 'grid'), parts along dimension 0, may hold values from -6 to 6
- pole_weight: float32 [4, 2], P('pole'), may hold values from -3 to 3
- ancestors: int32 [4, 10], replicated, may hold values from 0 to 15, all different within a row
Outputs:
- density_panel: float32 [8192, 1024], P(('ens', 'grid'), 'pole'), parts along dimension 0
- density_diagonal: float32 [2048, 256], P(('ens', 'grid')), parts along dimension 0
There are 2 independent parts, one for each index of `ens`. A program takes and returns all parts, laid end to end along the dimension named above; an argument that names none is the same for every part. Nothing has to cross between parts.
Inputs may be any that keep to these rules, and one draw needn't show every extreme that they name: `ancestors`: each row names 10 different ancestor blocks; every one of the 16 blocks is named by some row.
All inputs are finite; a program needn't handle non-finite values.
Results may differ from a plain program's by a relative error of at most 0.0022.
Values may be sent and summed in bfloat16 or wider, within the bound.
A program may use at most 128 MiB of HBM per device.

v0:
```python
import functools

import jax
import jax.numpy as jnp
from jax import lax
from jax.experimental import pallas as pl
from jax.experimental.pallas import tpu as pltpu
from jax.sharding import PartitionSpec as P

MESH = pl.DeviceIdType.MESH
HALVES = 2


def plain_product(left, right):
    return jnp.dot(left, right, preferred_element_type=jnp.float32)


def turned_product(left, right):
    return lax.dot_general(
        left, right, (((0,), (0,)), ((), ())), preferred_element_type=jnp.float32
    )


def portion_terms(rows_pair, block_index, offset, listed, factors, weights):
    tile_width = factors.shape[3]
    listed_count = factors.shape[1]
    height = rows_pair.shape[1]
    blocks = rows_pair.shape[2] // tile_width
    matches = listed == block_index

    def compute():
        chosen = rows_pair.reshape(2, height, blocks, tile_width)[:, :, listed, :].reshape(
            2, height, listed_count * tile_width
        )
        stacked = factors.reshape(2, listed_count * tile_width, tile_width)
        part_real = -(plain_product(chosen[0], stacked[0]) - plain_product(chosen[1], stacked[1]))
        part_imag = -(plain_product(chosen[0], stacked[1]) + plain_product(chosen[1], stacked[0]))
        panel_piece = weights[0] * part_imag + weights[1] * part_real
        rounded_real = part_real.astype(jnp.bfloat16)
        rounded_imag = part_imag.astype(jnp.bfloat16)
        position = jnp.sum(jnp.where(matches, jnp.arange(listed_count, dtype=jnp.int32), 0))
        matched = lax.dynamic_slice(
            factors, (jnp.int32(0), position, offset, jnp.int32(0)), (2, 1, height, tile_width)
        )[:, 0]
        diag_real = -(
            turned_product(matched[0], rounded_real) - turned_product(matched[1], rounded_imag)
        )
        diag_imag = -(
            turned_product(matched[0], rounded_imag) + turned_product(matched[1], rounded_real)
        )
        return (panel_piece, weights[0] * diag_imag + weights[1] * diag_real)

    def skipped():
        return (
            jnp.zeros((height, tile_width), jnp.float32),
            jnp.zeros((tile_width, tile_width), jnp.float32),
        )

    return lax.cond(jnp.any(matches), compute, skipped)


def rows_terms(rows_pair, row_first, listed, factors, weights):
    tile_width = factors.shape[3]
    height = rows_pair.shape[1]
    piece_rows = min(height, tile_width)
    panels = []
    diag_total = jnp.zeros((tile_width, tile_width), jnp.float32)
    for portion in range(height // piece_rows):
        row_start = row_first + portion * piece_rows
        panel_piece, diag_piece = portion_terms(
            rows_pair[:, portion * piece_rows : (portion + 1) * piece_rows],
            row_start // tile_width,
            row_start % tile_width,
            listed,
            factors,
            weights,
        )
        panels.append(panel_piece)
        diag_total = diag_total + diag_piece
    return (jnp.concatenate(panels, axis=0), diag_total)


def shards(inverse_pool, factor_tiles, diag_inverse, pole_weight, ancestors):
    device_index = lax.axis_index("grid")
    rows_here = inverse_pool.shape[2]
    supers = factor_tiles.shape[1]
    tile_width = factor_tiles.shape[5]
    row_slab = inverse_pool[0]
    weights = (pole_weight[0, 0], pole_weight[0, 1])
    row_first = device_index * rows_here
    own_panels = []
    diag_terms = []
    for supernode in range(supers):
        factors = lax.all_gather(factor_tiles[0, supernode], "grid", axis=2, tiled=True)
        listed = ancestors[supernode]
        own_panel, own_diag = rows_terms(row_slab, row_first, listed, factors, weights)
        diag_terms.append(own_diag)
        own_panels.append(own_panel)
    panel_rows = jnp.concatenate(own_panels, axis=1)
    panel_share = lax.psum_scatter(panel_rows, "pole", scatter_dimension=1, tiled=True)
    diag_term = jnp.stack(diag_terms, axis=0).reshape(supers * tile_width, tile_width)
    diag_local = diag_inverse[0]
    local_block = weights[0] * diag_local[1].astype(jnp.float32) + weights[1] * diag_local[
        0
    ].astype(jnp.float32)
    share_rows = local_block.shape[0]
    placed = lax.dynamic_update_slice(
        jnp.zeros_like(diag_term), local_block, (device_index * share_rows, jnp.int32(0))
    )
    spread = lax.psum_scatter(diag_term + placed, ("grid", "pole"), scatter_dimension=0, tiled=True)
    diag_share = lax.all_gather(spread, "pole", axis=0, tiled=True)
    return (panel_share, diag_share)


def fused_kernel(
    grid_size, pole_size, ancestors, weight, pool, tiles, diag_in,
    panel_out, diag_out,
    rows, sent_panel, got_panel, column, own_diag, diag_local, pole_sums, grid_send, grid_sums, final,
    pool_sem, tile_sem, diag_sem, up_sem, down_sem, arrive_sem,
    panel_send, panel_recv, a_send, a_recv, b_send, b_recv, c_send, c_recv, *factors,
):
    g = lax.axis_index("grid")
    q = lax.axis_index("pole")
    supers, listed_count = ancestors.shape
    half = factors[0].shape[3] // 2
    width = factors[0].shape[2]
    slice_rows = width // grid_size
    share = width // pole_size
    blocks = rows.shape[2] // width
    chunks = [(k, c) for k in range(supers) for c in range(HALVES)]

    tile_copies = []
    for j, (k, c) in enumerate(chunks):
        for part in range(2):
            copy = pltpu.make_async_copy(
                tiles.at[0, k, part, :, :, pl.ds(c * half, half)],
                factors[k].at[c, :, pl.ds(g * slice_rows, slice_rows), pl.ds(part * half, half)],
                tile_sem.at[j, part],
            )
            copy.start()
            tile_copies.append(copy)
    pool_copies = []
    for part in range(2):
        for a in range(rows.shape[1]):
            copy = pltpu.make_async_copy(
                pool.at[0, part, :, pl.ds(a * width, width)], rows.at[part, a], pool_sem.at[part, a]
            )
            copy.start()
            pool_copies.append(copy)
    diag_copy = pltpu.make_async_copy(diag_in.at[0], diag_local, diag_sem)
    diag_copy.start()

    barrier = pltpu.get_barrier_semaphore()
    for step in range(1, grid_size):
        pl.semaphore_signal(
            barrier, inc=1, device_id={"grid": lax.rem(g + step, grid_size)}, device_id_type=MESH
        )
    for step in range(1, pole_size):
        pl.semaphore_signal(
            barrier, inc=1, device_id={"pole": lax.rem(q + step, pole_size)}, device_id_type=MESH
        )
    pl.semaphore_wait(barrier, grid_size - 1 + pole_size - 1)

    def piece(j, source):
        k, c = chunks[j]
        return factors[k].at[c, :, pl.ds(source * slice_rows, slice_rows), :]

    def hop(j, source, up):
        return pltpu.make_async_remote_copy(
            src_ref=piece(j, source),
            dst_ref=piece(j, source),
            send_sem=(up_sem if up else down_sem).at[j, source],
            recv_sem=arrive_sem.at[j, source],
            device_id={"grid": g + 1 if up else g - 1},
            device_id_type=MESH,
        )

    def pass_on(j, distance):
        low = g - distance
        high = g + distance
        if distance:
            @pl.when(low >= 0)
            def _():
                hop(j, low, True).wait_recv()

        @pl.when(jnp.logical_and(low >= 0, g + 1 < grid_size))
        def _():
            hop(j, low, True).start()

        if distance:
            @pl.when(high < grid_size)
            def _():
                hop(j, high, False).wait_recv()

        @pl.when(jnp.logical_and(high < grid_size, g >= 1))
        def _():
            hop(j, high, False).start()

    for j in range(len(chunks)):
        tile_copies[2 * j].wait()
        tile_copies[2 * j + 1].wait()
        pass_on(j, 0)
    for copy in pool_copies:
        copy.wait()
    diag_copy.wait()
    for distance in range(1, grid_size - 1):
        for j in range(len(chunks)):
            pass_on(j, distance)

    w_real = weight[0, 0]
    w_imag = weight[0, 1]

    def panel_copy(j, k, c, slot):
        return pltpu.make_async_remote_copy(
            src_ref=sent_panel.at[k, c],
            dst_ref=got_panel.at[slot, c],
            send_sem=panel_send.at[j],
            recv_sem=panel_recv.at[slot, c],
            device_id={"pole": k},
            device_id_type=MESH,
        )

    def share_copy(k, r):
        return pltpu.make_async_remote_copy(
            src_ref=own_diag.at[k, pl.ds(r * share, share)],
            dst_ref=pole_sums.at[k, q],
            send_sem=a_send.at[k, r],
            recv_sem=a_recv.at[k, q],
            device_id={"pole": r},
            device_id_type=MESH,
        )

    def place_of(k, block):
        count = jnp.int32(0)
        position = jnp.int32(0)
        for n in range(listed_count):
            hit = (ancestors[k, n] == block).astype(jnp.int32)
            count = count + hit
            position = position + hit * n
        return count, jnp.clip(position, 0, listed_count - 1)

    for j, (k, c) in enumerate(chunks):
        pass_on(j, grid_size - 1)

        @pl.loop(0, blocks)
        def _(b):
            span = pl.ds(pl.multiple_of(b * width, width), width)
            with_real = jnp.zeros((width, 2 * half), jnp.float32)
            with_imag = jnp.zeros((width, 2 * half), jnp.float32)
            for n in range(listed_count):
                source = jnp.clip(ancestors[k, n], 0, rows.shape[1] - 1)
                factor = factors[k][c, n]
                with_real += jnp.dot(
                    rows[0, source, span, :], factor, preferred_element_type=jnp.float32
                )
                with_imag += jnp.dot(
                    rows[1, source, span, :], factor, preferred_element_type=jnp.float32
                )
            count, _ = place_of(k, g * blocks + b)
            keep = jnp.full((width, half), count, jnp.int32) > 0
            real = jnp.where(keep, with_imag[:, half:] - with_real[:, :half], 0.0)
            imag = jnp.where(keep, -(with_real[:, half:] + with_imag[:, :half]), 0.0)
            column[span, pl.ds(c * 2 * half, half)] = real.astype(jnp.bfloat16)
            column[span, pl.ds(c * 2 * half + half, half)] = imag.astype(jnp.bfloat16)
            term = w_real * imag + w_imag * real
            sent_panel[k, c, span, :] = term.astype(jnp.bfloat16)

            @pl.when(q == k)
            def _():
                panel_out[span, pl.ds(c * half, half)] = term

        @pl.when(q != k)
        def _():
            panel_copy(j, k, c, lax.rem(q - k + pole_size, pole_size) - 1).start()

        if c == HALVES - 1:
            for left in range(HALVES):
                for right in range(HALVES):
                    def add(b, total):
                        _, position = place_of(k, g * blocks + b)
                        span = pl.ds(pl.multiple_of(b * width, width), width)
                        return total + lax.dot_general(
                            factors[k][left, position],
                            column[span, pl.ds(right * 2 * half, 2 * half)],
                            (((0,), (0,)), ((), ())),
                            preferred_element_type=jnp.float32,
                        )

                    total = jnp.zeros((2 * half, 2 * half), jnp.float32)
                    for b in range(blocks):
                        total = add(b, total)
                    real = total[half:, half:] - total[:half, :half]
                    imag = -(total[:half, half:] + total[half:, :half])
                    own_diag[k, pl.ds(left * half, half), pl.ds(right * half, half)] = (
                        w_real * imag + w_imag * real
                    )

            @pl.when(g == k)
            def _():
                own_diag[k] = (
                    own_diag[k]
                    + w_real * diag_local[1].astype(jnp.float32)
                    + w_imag * diag_local[0].astype(jnp.float32)
                )

            pole_sums[k, q] = own_diag[k, pl.ds(pl.multiple_of(q * share, share), share), :]
            for r in range(pole_size):
                @pl.when(q != r)
                def _():
                    share_copy(k, r).start()

    def grid_copy(k):
        return pltpu.make_async_remote_copy(
            src_ref=grid_send.at[k],
            dst_ref=grid_sums.at[g],
            send_sem=b_send.at[k],
            recv_sem=b_recv.at[g],
            device_id={"grid": k},
            device_id_type=MESH,
        )

    def final_copy(r):
        mine = pl.ds(pl.multiple_of(q * share, share), share)
        return pltpu.make_async_remote_copy(
            src_ref=final.at[mine],
            dst_ref=final.at[mine],
            send_sem=c_send.at[r],
            recv_sem=c_recv.at[q],
            device_id={"pole": r},
            device_id_type=MESH,
        )

    def landing(buffer, semaphore):
        return pltpu.make_async_remote_copy(
            src_ref=buffer, dst_ref=buffer, send_sem=semaphore, recv_sem=semaphore,
            device_id={"pole": q}, device_id_type=MESH,
        )

    for k in range(supers):
        for r in range(pole_size):
            @pl.when(q != r)
            def _():
                landing(pole_sums.at[k, r], a_recv.at[k, r]).wait_recv()
        summed = pole_sums[k, 0]
        for r in range(1, pole_size):
            summed = summed + pole_sums[k, r]
        grid_send[k] = summed

        @pl.when(g != k)
        def _():
            grid_copy(k).start()

        @pl.when(g == k)
        def _():
            grid_sums[g] = grid_send[k]

    for s in range(grid_size):
        @pl.when(g != s)
        def _():
            landing(grid_sums.at[s], b_recv.at[s]).wait_recv()
    summed = grid_sums[0]
    for s in range(1, grid_size):
        summed = summed + grid_sums[s]
    final[pl.ds(pl.multiple_of(q * share, share), share), :] = summed
    for r in range(pole_size):
        @pl.when(q != r)
        def _():
            final_copy(r).start()

    for c in range(HALVES):
        for slot in range(pole_size - 1):
            landing(got_panel.at[slot, c], panel_recv.at[slot, c]).wait_recv()

        @pl.loop(0, blocks)
        def _(b):
            span = pl.ds(pl.multiple_of(b * width, width), width)
            lanes = pl.ds(c * half, half)
            total = panel_out[span, lanes]
            for slot in range(pole_size - 1):
                total = total + got_panel[slot, c, span, :].astype(jnp.float32)
            panel_out[span, lanes] = total

    for r in range(pole_size):
        @pl.when(q != r)
        def _():
            landing(final.at[pl.ds(r * share, share)], c_recv.at[r]).wait_recv()
    diag_out[...] = final[...]

    for distance in range(grid_size - 1):
        for j in range(len(chunks)):
            @pl.when(jnp.logical_and(g - distance >= 0, g + 1 < grid_size))
            def _():
                hop(j, g - distance, True).wait_send()

            @pl.when(jnp.logical_and(g + distance < grid_size, g >= 1))
            def _():
                hop(j, g + distance, False).wait_send()
    for j, (k, c) in enumerate(chunks):
        @pl.when(q != k)
        def _():
            panel_copy(j, k, c, lax.rem(q - k + pole_size, pole_size) - 1).wait_send()
    for k in range(supers):
        for r in range(pole_size):
            @pl.when(q != r)
            def _():
                share_copy(k, r).wait_send()

        @pl.when(g != k)
        def _():
            grid_copy(k).wait_send()
    for r in range(pole_size):
        @pl.when(q != r)
        def _():
            final_copy(r).wait_send()


def fused(grid_size, pole_size, inverse_pool, factor_tiles, diag_inverse, pole_weight, ancestors):
    supers, listed_count = ancestors.shape
    width = factor_tiles.shape[5]
    height = inverse_pool.shape[2]
    half = width // HALVES
    share = width // pole_size
    chunks = supers * HALVES
    dma = pltpu.SemaphoreType.DMA
    f32 = jnp.float32
    bf16 = jnp.bfloat16
    scratch = [
        pltpu.VMEM((2, inverse_pool.shape[3] // width, height, width), bf16),
        pltpu.VMEM((supers, HALVES, height, half), bf16),
        pltpu.VMEM((pole_size - 1, HALVES, height, half), bf16),
        pltpu.VMEM((height, 2 * width), bf16),
        pltpu.VMEM((supers, width, width), f32),
        pltpu.VMEM(diag_inverse.shape[1:], bf16),
        pltpu.VMEM((supers, pole_size, share, width), f32),
        pltpu.VMEM((supers, share, width), f32),
        pltpu.VMEM((grid_size, share, width), f32),
        pltpu.VMEM((width, width), f32),
        dma((2, inverse_pool.shape[3] // width)), dma((chunks, 2)), dma(()),
        dma((chunks, grid_size)), dma((chunks, grid_size)), dma((chunks, grid_size)),
        dma((chunks,)), dma((pole_size - 1, HALVES)),
        dma((supers, pole_size)), dma((supers, pole_size)),
        dma((supers,)), dma((grid_size,)),
        dma((pole_size,)), dma((pole_size,)),
    ] + [pltpu.VMEM((HALVES, listed_count, width, 2 * half), bf16)] * supers
    smem = pl.BlockSpec(memory_space=pltpu.SMEM)
    vmem = pl.BlockSpec(memory_space=pltpu.VMEM)
    anywhere = pl.BlockSpec(memory_space=pl.ANY)
    return pl.pallas_call(
        functools.partial(fused_kernel, grid_size, pole_size),
        out_shape=(
            jax.ShapeDtypeStruct((height, width), f32),
            jax.ShapeDtypeStruct((width, width), f32),
        ),
        in_specs=[smem, smem, anywhere, anywhere, anywhere],
        out_specs=(vmem, vmem),
        scratch_shapes=scratch,
        compiler_params=pltpu.CompilerParams(
            collective_id=0, has_side_effects=True, vmem_limit_bytes=56 * 2**20
        ),
    )(ancestors, pole_weight, inverse_pool, factor_tiles, diag_inverse)


def choose(grid_size, pole_size, inverse_pool, factor_tiles, diag_inverse, pole_weight, ancestors):
    supers = ancestors.shape[0]
    width = factor_tiles.shape[5]
    whole_blocks = inverse_pool.shape[2] % width == 0 and factor_tiles.shape[4] % 16 == 0
    if whole_blocks and supers == grid_size == pole_size and width % (HALVES * 128) == 0:
        return fused(
            grid_size, pole_size, inverse_pool, factor_tiles, diag_inverse, pole_weight, ancestors
        )
    return shards(inverse_pool, factor_tiles, diag_inverse, pole_weight, ancestors)


def solution(mesh):
    in_specs = (
        P(("ens", "pole"), None, "grid", None),
        P(("ens", "pole"), None, None, None, "grid", None),
        P(("ens", "pole"), None, "grid", None),
        P("pole", None),
        P(),
    )
    out_specs = (P(("ens", "grid"), "pole"), P(("ens", "grid"), None))
    body = functools.partial(choose, mesh.shape["grid"], mesh.shape["pole"])
    return jax.shard_map(body, mesh=mesh, in_specs=in_specs, out_specs=out_specs, check_vma=False)
```

profile of v0, /device:TPU:29, one launch (start us, length us, event | category | flops | bytes accessed | tf_op | source)
XLA Modules:
  0.0 203.2 jit_solution(9359327193875326488)
XLA Ops:
  0.6 198.7 %shard_map.68 = (f32[1024,256]{1,0:T(8,128)}, f32[256,256]{1,0:T(8,128)}) custom-call(s32[4,10]{1,0:T(4,128)} %ancestors.1, f32[1,2]{1,0:T(1,128)} %weight.1, bf16[1,2,1024,4096]{3,2,1,0:T(8,128)(2,1)} %pool.1, bf16[1,4,2,10,64,256]{5,4,3,2,1,0:T(8,128)(2,1)} %tiles.1, bf16[1,2,256,256]{3,2,1,0:T(8,128)(2,1)} %diag_in.1), custom_call_target="tpu_custom_call" | custom-call | tf_op jit(solution)/shard_map/pallas_call | solution.py:448
  199.3 2.3 %copy.9 = f32[1024,256]{1,0:T(8,128)} copy(f32[1024,256]{1,0:T(8,128)} %get-tuple-element.4) | data formatting | bytes 2097152
  201.6 1.7 copy.10
where the time goes:
time: 203 us
  Pallas kernels  199 us (98%)
  local copies, waits for them, and re-layouts  3.93 us (2%)
    pallas_call x1, Pallas kernels, fused(): pl.pallas_call(functools.partial(fused_kernel, grid_size, pole_size), out...  199 us

commit v1 on v0

--- a/solution.py
+++ b/solution.py
@@ -115,7 +115,7 @@
 def fused_kernel(
     grid_size, pole_size, ancestors, weight, pool, tiles, diag_in,
     panel_out, diag_out,
-    rows, sent_panel, got_panel, column, own_diag, diag_local, pole_sums, grid_send, grid_sums, final,
+    rows, sent_panel, got_panel, column, own_diag, sent_diag, diag_local, pole_sums, grid_send, grid_sums, final,
     pool_sem, tile_sem, diag_sem, up_sem, down_sem, arrive_sem,
     panel_send, panel_recv, a_send, a_recv, b_send, b_recv, c_send, c_recv, *factors,
 ):
@@ -210,19 +210,21 @@
     w_real = weight[0, 0]
     w_imag = weight[0, 1]
 
-    def panel_copy(j, k, c, slot):
-        return pltpu.make_async_remote_copy(
-            src_ref=sent_panel.at[k, c],
-            dst_ref=got_panel.at[slot, c],
-            send_sem=panel_send.at[j],
-            recv_sem=panel_recv.at[slot, c],
+    def panel_copy(j, k, c, b):
+        slot = lax.rem(q - k + pole_size, pole_size) - 1
+        span = pl.ds(b * width, width)
+        return pltpu.make_async_remote_copy(
+            src_ref=sent_panel.at[k, c, span],
+            dst_ref=got_panel.at[slot, c, span],
+            send_sem=panel_send.at[j, b],
+            recv_sem=panel_recv.at[slot, c, b],
             device_id={"pole": k},
             device_id_type=MESH,
         )
 
     def share_copy(k, r):
         return pltpu.make_async_remote_copy(
-            src_ref=own_diag.at[k, pl.ds(r * share, share)],
+            src_ref=sent_diag.at[k, pl.ds(r * share, share)],
             dst_ref=pole_sums.at[k, q],
             send_sem=a_send.at[k, r],
             recv_sem=a_recv.at[k, q],
@@ -238,6 +240,51 @@
             count = count + hit
             position = position + hit * n
         return count, jnp.clip(position, 0, listed_count - 1)
+
+    def grid_copy(k):
+        return pltpu.make_async_remote_copy(
+            src_ref=grid_send.at[k],
+            dst_ref=grid_sums.at[g],
+            send_sem=b_send.at[k],
+            recv_sem=b_recv.at[g],
+            device_id={"grid": k},
+            device_id_type=MESH,
+        )
+
+    def final_copy(r):
+        mine = pl.ds(pl.multiple_of(q * share, share), share)
+        return pltpu.make_async_remote_copy(
+            src_ref=final.at[mine],
+            dst_ref=final.at[mine],
+            send_sem=c_send.at[r],
+            recv_sem=c_recv.at[q],
+            device_id={"pole": r},
+            device_id_type=MESH,
+        )
+
+    def landing(buffer, semaphore):
+        return pltpu.make_async_remote_copy(
+            src_ref=buffer, dst_ref=buffer, send_sem=semaphore, recv_sem=semaphore,
+            device_id={"pole": q}, device_id_type=MESH,
+        )
+
+    def to_owner(k):
+        for r in range(pole_size):
+            @pl.when(q != r)
+            def _():
+                landing(pole_sums.at[k, r], a_recv.at[k, r]).wait_recv()
+        summed = own_diag[k, pl.ds(pl.multiple_of(q * share, share), share), :]
+        for step in range(1, pole_size):
+            summed = summed + pole_sums[k, lax.rem(q + step, pole_size)].astype(jnp.float32)
+        grid_send[k] = summed
+
+        @pl.when(g != k)
+        def _():
+            grid_copy(k).start()
+
+        @pl.when(g == k)
+        def _():
+            grid_sums[g] = grid_send[k]
 
     for j, (k, c) in enumerate(chunks):
         pass_on(j, grid_size - 1)
@@ -269,9 +316,9 @@
             def _():
                 panel_out[span, pl.ds(c * half, half)] = term
 
-        @pl.when(q != k)
-        def _():
-            panel_copy(j, k, c, lax.rem(q - k + pole_size, pole_size) - 1).start()
+            @pl.when(q != k)
+            def _():
+                panel_copy(j, k, c, b).start()
 
         if c == HALVES - 1:
             for left in range(HALVES):
@@ -303,57 +350,16 @@
                     + w_imag * diag_local[0].astype(jnp.float32)
                 )
 
-            pole_sums[k, q] = own_diag[k, pl.ds(pl.multiple_of(q * share, share), share), :]
+            sent_diag[k] = own_diag[k].astype(jnp.bfloat16)
             for r in range(pole_size):
                 @pl.when(q != r)
                 def _():
                     share_copy(k, r).start()
 
-    def grid_copy(k):
-        return pltpu.make_async_remote_copy(
-            src_ref=grid_send.at[k],
-            dst_ref=grid_sums.at[g],
-            send_sem=b_send.at[k],
-            recv_sem=b_recv.at[g],
-            device_id={"grid": k},
-            device_id_type=MESH,
-        )
-
-    def final_copy(r):
-        mine = pl.ds(pl.multiple_of(q * share, share), share)
-        return pltpu.make_async_remote_copy(
-            src_ref=final.at[mine],
-            dst_ref=final.at[mine],
-            send_sem=c_send.at[r],
-            recv_sem=c_recv.at[q],
-            device_id={"pole": r},
-            device_id_type=MESH,
-        )
-
-    def landing(buffer, semaphore):
-        return pltpu.make_async_remote_copy(
-            src_ref=buffer, dst_ref=buffer, send_sem=semaphore, recv_sem=semaphore,
-            device_id={"pole": q}, device_id_type=MESH,
-        )
-
-    for k in range(supers):
-        for r in range(pole_size):
-            @pl.when(q != r)
-            def _():
-                landing(pole_sums.at[k, r], a_recv.at[k, r]).wait_recv()
-        summed = pole_sums[k, 0]
-        for r in range(1, pole_size):
-            summed = summed + pole_sums[k, r]
-        grid_send[k] = summed
-
-        @pl.when(g != k)
-        def _():
-            grid_copy(k).start()
-
-        @pl.when(g == k)
-        def _():
-            grid_sums[g] = grid_send[k]
-
+            if k:
+                to_owner(k - 1)
+
+    to_owner(supers - 1)
     for s in range(grid_size):
         @pl.when(g != s)
         def _():
@@ -368,12 +374,11 @@
             final_copy(r).start()
 
     for c in range(HALVES):
-        for slot in range(pole_size - 1):
-            landing(got_panel.at[slot, c], panel_recv.at[slot, c]).wait_recv()
-
         @pl.loop(0, blocks)
         def _(b):
             span = pl.ds(pl.multiple_of(b * width, width), width)
+            for slot in range(pole_size - 1):
+                landing(got_panel.at[slot, c, span], panel_recv.at[slot, c, b]).wait_recv()
             lanes = pl.ds(c * half, half)
             total = panel_out[span, lanes]
             for slot in range(pole_size - 1):
@@ -396,9 +401,10 @@
             def _():
                 hop(j, g + distance, False).wait_send()
     for j, (k, c) in enumerate(chunks):
-        @pl.when(q != k)
-        def _():
-            panel_copy(j, k, c, lax.rem(q - k + pole_size, pole_size) - 1).wait_send()
+        for b in range(blocks):
+            @pl.when(q != k)
+            def _():
+                panel_copy(j, k, c, b).wait_send()
     for k in range(supers):
         for r in range(pole_size):
             @pl.when(q != r)
@@ -421,6 +427,7 @@
     half = width // HALVES
     share = width // pole_size
     chunks = supers * HALVES
+    blocks = height // width
     dma = pltpu.SemaphoreType.DMA
     f32 = jnp.float32
     bf16 = jnp.bfloat16
@@ -430,14 +437,15 @@
         pltpu.VMEM((pole_size - 1, HALVES, height, half), bf16),
         pltpu.VMEM((height, 2 * width), bf16),
         pltpu.VMEM((supers, width, width), f32),
+        pltpu.VMEM((supers, width, width), bf16),
         pltpu.VMEM(diag_inverse.shape[1:], bf16),
-        pltpu.VMEM((supers, pole_size, share, width), f32),
+        pltpu.VMEM((supers, pole_size, share, width), bf16),
         pltpu.VMEM((supers, share, width), f32),
         pltpu.VMEM((grid_size, share, width), f32),
         pltpu.VMEM((width, width), f32),
         dma((2, inverse_pool.shape[3] // width)), dma((chunks, 2)), dma(()),
         dma((chunks, grid_size)), dma((chunks, grid_size)), dma((chunks, grid_size)),
-        dma((chunks,)), dma((pole_size - 1, HALVES)),
+        dma((chunks, blocks)), dma((pole_size - 1, HALVES, blocks)),
         dma((supers, pole_size)), dma((supers, pole_size)),
         dma((supers,)), dma((grid_size,)),
         dma((pole_size,)), dma((pole_size,)),

time: 203 us -> 201 us (level)
  Pallas kernels: 199 us -> 196 us
    pallas_call x1, Pallas kernels: 199 us -> 196 us  [fused(): pl.pallas_call(functools.partial(fused_kernel, grid_size, pole_size), out...]
where the time goes in v1:
time: 201 us; the launch traced here: 200 us
  Pallas kernels  196 us (98%)
  local copies, waits for them, and re-layouts  3.93 us (2%)
    pallas_call x1, Pallas kernels, fused(): pl.pallas_call(functools.partial(fused_kernel, grid_size, pole_size), out...  196 us

profile of v1, /device:TPU:29, one launch (start us, length us, event | category | flops | bytes accessed | tf_op | source)
XLA Modules:
  0.0 200.4 jit_solution(15287391734290388883)
XLA Ops:
  0.6 195.8 %shard_map.68 = (f32[1024,256]{1,0:T(8,128)}, f32[256,256]{1,0:T(8,128)}) custom-call(s32[4,10]{1,0:T(4,128)} %ancestors.1, f32[1,2]{1,0:T(1,128)} %weight.1, bf16[1,2,1024,4096]{3,2,1,0:T(8,128)(2,1)} %pool.1, bf16[1,4,2,10,64,256]{5,4,3,2,1,0:T(8,128)(2,1)} %tiles.1, bf16[1,2,256,256]{3,2,1,0:T(8,128)(2,1)} %diag_in.1), custom_call_target="tpu_custom_call" | custom-call | tf_op jit(solution)/shard_map/pallas_call | solution.py:456
  196.5 2.3 %copy.9 = f32[1024,256]{1,0:T(8,128)} copy(f32[1024,256]{1,0:T(8,128)} %get-tuple-element.4) | data formatting | bytes 2097152
  198.7 1.7 copy.10

commit v2 on v1

--- a/solution.py
+++ b/solution.py
@@ -139,6 +139,59 @@
             )
             copy.start()
             tile_copies.append(copy)
+    diag_copy = pltpu.make_async_copy(diag_in.at[0], diag_local, diag_sem)
+    diag_copy.start()
+
+    barrier = pltpu.get_barrier_semaphore()
+    for step in range(1, grid_size):
+        pl.semaphore_signal(
+            barrier, inc=1, device_id={"grid": lax.rem(g + step, grid_size)}, device_id_type=MESH
+        )
+    for step in range(1, pole_size):
+        pl.semaphore_signal(
+            barrier, inc=1, device_id={"pole": lax.rem(q + step, pole_size)}, device_id_type=MESH
+        )
+    pl.semaphore_wait(barrier, grid_size - 1 + pole_size - 1)
+
+    def piece(j, source):
+        k, c = chunks[j]
+        return factors[k].at[c, :, pl.ds(source * slice_rows, slice_rows), :]
+
+    def hop(j, source, up):
+        return pltpu.make_async_remote_copy(
+            src_ref=piece(j, source),
+            dst_ref=piece(j, source),
+            send_sem=(up_sem if up else down_sem).at[j, source],
+            recv_sem=arrive_sem.at[j, source],
+            device_id={"grid": g + 1 if up else g - 1},
+            device_id_type=MESH,
+        )
+
+    def pass_on(j, distance):
+        low = g - distance
+        high = g + distance
+        if distance:
+            @pl.when(low >= 0)
+            def _():
+                hop(j, low, True).wait_recv()
+
+        @pl.when(jnp.logical_and(low >= 0, g + 1 < grid_size))
+        def _():
+            hop(j, low, True).start()
+
+        if distance:
+            @pl.when(high < grid_size)
+            def _():
+                hop(j, high, False).wait_recv()
+
+        @pl.when(jnp.logical_and(high < grid_size, g >= 1))
+        def _():
+            hop(j, high, False).start()
+
+    for j in range(len(chunks)):
+        tile_copies[2 * j].wait()
+        tile_copies[2 * j + 1].wait()
+        pass_on(j, 0)
     pool_copies = []
     for part in range(2):
         for a in range(rows.shape[1]):
@@ -147,65 +200,12 @@
             )
             copy.start()
             pool_copies.append(copy)
-    diag_copy = pltpu.make_async_copy(diag_in.at[0], diag_local, diag_sem)
-    diag_copy.start()
-
-    barrier = pltpu.get_barrier_semaphore()
-    for step in range(1, grid_size):
-        pl.semaphore_signal(
-            barrier, inc=1, device_id={"grid": lax.rem(g + step, grid_size)}, device_id_type=MESH
-        )
-    for step in range(1, pole_size):
-        pl.semaphore_signal(
-            barrier, inc=1, device_id={"pole": lax.rem(q + step, pole_size)}, device_id_type=MESH
-        )
-    pl.semaphore_wait(barrier, grid_size - 1 + pole_size - 1)
-
-    def piece(j, source):
-        k, c = chunks[j]
-        return factors[k].at[c, :, pl.ds(source * slice_rows, slice_rows), :]
-
-    def hop(j, source, up):
-        return pltpu.make_async_remote_copy(
-            src_ref=piece(j, source),
-            dst_ref=piece(j, source),
-            send_sem=(up_sem if up else down_sem).at[j, source],
-            recv_sem=arrive_sem.at[j, source],
-            device_id={"grid": g + 1 if up else g - 1},
-            device_id_type=MESH,
-        )
-
-    def pass_on(j, distance):
-        low = g - distance
-        high = g + distance
-        if distance:
-            @pl.when(low >= 0)
-            def _():
-                hop(j, low, True).wait_recv()
-
-        @pl.when(jnp.logical_and(low >= 0, g + 1 < grid_size))
-        def _():
-            hop(j, low, True).start()
-
-        if distance:
-            @pl.when(high < grid_size)
-            def _():
-                hop(j, high, False).wait_recv()
-
-        @pl.when(jnp.logical_and(high < grid_size, g >= 1))
-        def _():
-            hop(j, high, False).start()
-
-    for j in range(len(chunks)):
-        tile_copies[2 * j].wait()
-        tile_copies[2 * j + 1].wait()
-        pass_on(j, 0)
+    for distance in range(1, grid_size - 1):
+        for j in range(len(chunks)):
+            pass_on(j, distance)
     for copy in pool_copies:
         copy.wait()
     diag_copy.wait()
-    for distance in range(1, grid_size - 1):
-        for j in range(len(chunks)):
-            pass_on(j, distance)
 
     w_real = weight[0, 0]
     w_imag = weight[0, 1]

time: 201 us -> 201 us (level)
  no operation moved by 1% of the time
where the time goes in v2:
time: 201 us; the launch traced here: 200 us
  Pallas kernels  196 us (98%)
  local copies, waits for them, and re-layouts  3.93 us (2%)
    pallas_call x1, Pallas kernels, fused(): pl.pallas_call(functools.partial(fused_kernel, grid_size, pole_size), out...  196 us

profile of v2, /device:TPU:29, one launch (start us, length us, event | category | flops | bytes accessed | tf_op | source)
XLA Modules:
  0.0 200.4 jit_solution(11761488176701533107)
XLA Ops:
  0.6 195.8 %shard_map.68 = (f32[1024,256]{1,0:T(8,128)}, f32[256,256]{1,0:T(8,128)}) custom-call(s32[4,10]{1,0:T(4,128)} %ancestors.1, f32[1,2]{1,0:T(1,128)} %weight.1, bf16[1,2,1024,4096]{3,2,1,0:T(8,128)(2,1)} %pool.1, bf16[1,4,2,10,64,256]{5,4,3,2,1,0:T(8,128)(2,1)} %tiles.1, bf16[1,2,256,256]{3,2,1,0:T(8,128)(2,1)} %diag_in.1), custom_call_target="tpu_custom_call" | custom-call | tf_op jit(solution)/shard_map/pallas_call | solution.py:456
  196.4 2.3 %copy.9 = f32[1024,256]{1,0:T(8,128)} copy(f32[1024,256]{1,0:T(8,128)} %get-tuple-element.4) | data formatting | bytes 2097152
  198.7 1.7 copy.10
